TPU v7x, 256 devices: a whole 4x4x8 slice. The times are simulated.
256 devices in a mesh: row: 8 (over z), col: 32 (over y, x, core).
Axes of the slice: x: 4, y: 4, z: 8, core: 2. Of those that a mesh axis runs over, the one named last changes fastest.
Arguments:
- ancestor_inverse: bfloat16 [24576, 24576], P('row', 'col'), may hold values from -6 to 6
- factor_slots: bfloat16 [3, 16384, 512], P(None, ('row', 'col')), may hold values from -0.25 to 0.25
- slot_tiles: int32 [3, 64], replicated, may hold values from -1 to 95, as said below
- parent_factor: bfloat16 [2, 512, 512], replicated, may hold values from -0.25 to 0.25
- diag_inverse: float32 [3, 512, 512], replicated, may hold values from -6 to 6
Outputs:
- inverse_panels: bfloat16 [3, 24576, 512], P(None, ('row', 'col'))
- diag_blocks: float32 [3, 512, 512], replicated
- parent_blocks: float32 [2, 512, 512], replicated
Inputs may be any that keep to these rules, and one draw needn't show every extreme that they name: `slot_tiles`: entries b * 2 to b * 2 + 1 of a supernode's row are the slots of column block b: each is -1 (empty) or names a tile from b * 3 to b * 3 + 2, no tile twice; in each supernode some block has all its slots filled. `factor_slots`: rows of an empty slot are not part of the factor.
All inputs are finite; a program needn't handle non-finite values.
Results may differ from a plain program's by a relative error of at most 0.00075.
Values may be sent and summed in bfloat16 or wider, within the bound.
No kernel may reach another device: no remote copies, remote signals or barrier semaphores. Data moves between devices by JAX's collectives and lax.ppermute only.
A program may use at most 128 MiB of HBM per device.

v0:
```python
import jax
import jax.numpy as jnp
from jax import lax
from jax.sharding import PartitionSpec as P

TILE = 256
CAP = 2
exact_mode = lax.Precision.HIGHEST


def spread(shard, axis, root):
    mine = lax.axis_index(axis) == root
    return lax.psum(jnp.where(mine, shard, jnp.zeros_like(shard)), axis)


def padded_block(slot_data, slot_ids, block_index, tiles_per_block, tile_rows):
    local_tile = slot_ids - block_index * tiles_per_block
    pieces = []
    for tile_index in range(tiles_per_block):
        chosen = jnp.zeros((tile_rows, slot_data.shape[1]), slot_data.dtype)
        for member in range(slot_ids.shape[0]):
            chosen = jnp.where(
                local_tile[member] == tile_index,
                slot_data[member * tile_rows : (member + 1) * tile_rows],
                chosen,
            )
        pieces.append(chosen)
    return jnp.concatenate(pieces, axis=0)


def chosen_columns(inverse_block, slot_ids, block_index, tiles_per_block, tile_rows):
    local_tile = jnp.clip(slot_ids - block_index * tiles_per_block, 0, tiles_per_block - 1)
    pieces = [
        lax.dynamic_slice_in_dim(inverse_block, local_tile[member] * tile_rows, tile_rows, 1)
        for member in range(slot_ids.shape[0])
    ]
    return jnp.concatenate(pieces, axis=1)


def masked_rows(slot_data, slot_ids, tile_rows):
    live_rows = jnp.repeat(slot_ids >= 0, tile_rows)
    return jnp.where(live_rows[:, None], slot_data, jnp.zeros_like(slot_data))


def on_device(ancestor_inverse, factor_slots, slot_tiles, parent_factor, diag_inverse):
    row_count = lax.axis_size("row")
    col_count = lax.axis_size("col")
    row_index = lax.axis_index("row")
    col_index = lax.axis_index("col")
    block_rows, block_cols = ancestor_inverse.shape
    tile_rows = TILE
    tiles_per_block = block_cols // tile_rows
    node_count = factor_slots.shape[0]
    slot_count = CAP
    slot_rows = slot_count * tile_rows
    groups_per_row = col_count // row_count
    panel_rows = block_rows // col_count
    own_block = row_index * groups_per_row + col_index // row_count
    own_offset = col_index % row_count * panel_rows
    slot_start = col_index % groups_per_row * slot_rows
    owner_row = col_index // groups_per_row

    def finish(node, first_total, second_total, prev_diag):
        if node == 0:
            return (diag_inverse[0] - first_total, None)
        parent_link = parent_factor[node - 1].astype(jnp.float32)
        upper = -(second_total + jnp.dot(prev_diag, parent_link, precision=exact_mode))
        diagonal = (
            diag_inverse[node] - first_total - jnp.dot(parent_link.T, upper, precision=exact_mode)
        )
        return (diagonal, upper)

    def node_sums(node, first_part, second_part):
        if node == 0:
            return (lax.psum(first_part, ("row", "col")), None)
        return lax.psum((first_part, second_part), ("row", "col"))

    panels = []
    diagonals = []
    parents = []
    previous = None
    prev_diag = None
    for node in range(node_count):
        row_slots = lax.all_gather(factor_slots[node], "col", axis=0, tiled=True)
        mine = lax.dynamic_slice_in_dim(row_slots, slot_start, slot_rows, 0)
        col_slots = spread(mine, "row", owner_row)
        tiles_node = slot_tiles[node]
        col_ids = lax.dynamic_slice_in_dim(tiles_node, col_index * slot_count, slot_count)
        prepare_columns = chosen_columns(
            ancestor_inverse, col_ids, col_index, tiles_per_block, tile_rows
        )
        prepare_weights = masked_rows(col_slots, col_ids, tile_rows)
        own_ids = lax.dynamic_slice_in_dim(tiles_node, own_block * slot_count, slot_count)
        own_slots = lax.dynamic_slice_in_dim(
            row_slots, col_index // row_count * slot_rows, slot_rows, 0
        )
        own_padded = padded_block(own_slots, own_ids, own_block, tiles_per_block, tile_rows)
        own_rows = lax.dynamic_slice_in_dim(own_padded, own_offset, panel_rows, 0)
        row_padded = None
        columns, weights, own_rows, row_padded = (
            prepare_columns,
            prepare_weights,
            own_rows.astype(jnp.float32),
            row_padded,
        )
        second_part = None
        if node > 0:
            second_part = jnp.dot(previous.T, own_rows, precision=exact_mode)
        summed = lax.psum_scatter(
            jnp.dot(columns, weights, preferred_element_type=jnp.float32),
            "col",
            scatter_dimension=0,
            tiled=True,
        )
        column = -summed
        if node > 0:
            advance_parent_link = parent_factor[node - 1].astype(jnp.float32)
            column = column - jnp.dot(previous, advance_parent_link, precision=exact_mode)
        first_part = jnp.dot(own_rows.T, column, precision=exact_mode)
        first_total, second_total = node_sums(node, first_part, second_part)
        diagonal, upper = finish(node, first_total, second_total, prev_diag)
        panels.append(column.astype(jnp.bfloat16))
        diagonals.append(diagonal)
        if node > 0:
            parents.append(upper)
        previous = column
        prev_diag = diagonal
    return (jnp.stack(panels), jnp.stack(diagonals), jnp.stack(parents))


def solution(mesh):
    placed = (P("row", "col"), P(None, ("row", "col"), None), P(), P(), P())
    return jax.shard_map(
        on_device,
        mesh=mesh,
        in_specs=placed,
        out_specs=(P(None, ("row", "col"), None), P(), P()),
        check_vma=False,
    )
```

profile of v0, /device:TPU:8, one launch (start us, length us, event | category | flops | bytes accessed | tf_op | source)
XLA Modules:
  0.0 841.9 jit_solution(13287973406344088835)
XLA Ops:
  10.4 51.9 %all-gather.9.cloned.1.call-done = bf16[1,2048,512]{2,1,0:T(8,128)(2,1)} async-done(((bf16[1,64,512]{2,1,0:T(8,128)(2,1)}), bf16[1,2048,512]{2,1,0:T(8,128)(2,1)}) %all-gather.9.cloned.1.call-update) | async-done | bytes 2097168 | tf_op jit(solution)/shard_map/all_gather | solution.py:84
  62.3 1.9 select_bitcast_fusion.1
  64.2 49.2 %all-gather.7.cloned.1.call-done = bf16[1,2048,512]{2,1,0:T(8,128)(2,1)} async-done(((bf16[1,64,512]{2,1,0:T(8,128)(2,1)}), bf16[1,2048,512]{2,1,0:T(8,128)(2,1)}) %all-gather.7.cloned.1.call-update) | async-done | bytes 2097168 | tf_op jit(solution)/shard_map/all_gather | solution.py:84
  113.4 1.9 select_bitcast_fusion.2
  115.3 49.2 %all-gather.11.cloned.1.call-done = bf16[1,2048,512]{2,1,0:T(8,128)(2,1)} async-done(((bf16[1,64,512]{2,1,0:T(8,128)(2,1)}), bf16[1,2048,512]{2,1,0:T(8,128)(2,1)}) %all-gather.11.cloned.1.call-update) | async-done | bytes 2097168 | tf_op jit(solution)/shard_map/all_gather | solution.py:84
  164.5 1.9 select_bitcast_fusion
  172.6 6.8 constant_dynamic-slice_fusion.4
  179.5 66.0 %all-reduce.7.cloned.1.call-done = (bf16[512,512]{1,0:T(8,128)(2,1)}, bf16[512,512]{1,0:T(8,128)(2,1)}, bf16[512,512]{1,0:T(8,128)(2,1)}) async-done(((bf16[512,512]{1,0:T(8,128)(2,1)}, bf16[512,512]{1,0:T(8,128)(2,1)}, bf16[512,512]{1,0:T(8,128)(2,1)}), (bf16[512,512]{1,0:T(8,128)(2,1)}, bf16[512,512]{1,0:T(8,128)(2,1)}, bf16[512,512]{1,0:T(8,128)(2,1)})) %all-reduce.7.cloned.1.call-update) | async-done | bytes 1572880 | tf_op jit(solution)/shard_map/psum | solution.py:13
  245.4 6.5 fusion.4
  252.2 6.5 fusion
  258.8 5.5 fusion.8
  278.5 2.0 select_bitcast_fusion.10
  281.7 63.3 %reduce-scatter.6.cloned.1.call-done = f32[96,512]{1,0:T(8,128)} async-done(((f32[3072,512]{1,0:T(8,128)}), f32[96,512]{1,0:T(8,128)}) %reduce-scatter.6.cloned.1.call-update) | async-done | bytes 196624 | tf_op jit(solution)/shard_map/reduce_scatter | solution.py:109
  345.0 97.1 %reduce-scatter.4.cloned.1.call-done = f32[96,512]{1,0:T(8,128)} async-done(((f32[3072,512]{1,0:T(8,128)}), f32[96,512]{1,0:T(8,128)}) %reduce-scatter.4.cloned.1.call-update) | async-done | bytes 196624 | tf_op jit(solution)/shard_map/reduce_scatter | solution.py:109
  443.5 1.7 fusion.69
  445.2 94.2 %reduce-scatter.8.cloned.1.call-done = f32[96,512]{1,0:T(8,128)} async-done(((f32[3072,512]{1,0:T(8,128)}), f32[96,512]{1,0:T(8,128)}) %reduce-scatter.8.cloned.1.call-update) | async-done | bytes 196624 | tf_op jit(solution)/shard_map/reduce_scatter | solution.py:109
  540.7 1.7 fusion.67
  542.5 1.7 fusion.64
  544.2 1.7 fusion.39
  545.8 1.8 fusion.41
  548.5 274.5 %all-reduce.5.cloned.1.call-done = (f32[512,512]{1,0:T(8,128)}, f32[512,512]{1,0:T(8,128)}, f32[512,512]{1,0:T(8,128)}, f32[512,512]{1,0:T(8,128)}, f32[512,512]{1,0:T(8,128)}) async-done(((f32[512,512]{1,0:T(8,128)}, f32[512,512]{1,0:T(8,128)}, f32[512,512]{1,0:T(8,128)}, f32[512,512]{1,0:T(8,128)}, f32[512,512]{1,0:T(8,128)}), (f32[512,512]{1,0:T(8,128)}, f32[512,512]{1,0:T(8,128)}, f32[512,512]{1,0:T(8,128)}, ...) | async-done | bytes 5242896 | tf_op jit(solution)/shard_map/psum | solution.py:76
  823.1 1.9 fusion.29
  825.6 2.6 fusion.13
  833.0 2.0 pad_maximum_fusion
  (63 shorter events, 18.7 us)
Async XLA Ops:
  7.2 159.4 %copy-start.8 = (s32[3,64]{1,0:T(4,128)S(1)}, s32[3,64]{1,0:T(4,128)}, u32[]{:S(2)}) copy-start(s32[3,64]{1,0:T(4,128)} %param.7) | copy-start | bytes 2308
  7.2 55.1 %all-gather.9.cloned.1.call-start = ((), (), s32[]{:S(2)}) async-start(), calls=%async_computation.7 | async-start | bytes 2162688 | tf_op jit(solution)/shard_map/all_gather | solution.py:84
  8.8 104.6 %all-gather.7.cloned.1.call-start = ((), (), s32[]{:S(2)}) async-start(), calls=%async_computation.6 | async-start | bytes 2162688 | tf_op jit(solution)/shard_map/all_gather | solution.py:84
  9.6 154.9 %all-gather.11.cloned.1.call-start = ((), (), s32[]{:S(2)}) async-start(), calls=%async_computation.8 | async-start | bytes 2162688 | tf_op jit(solution)/shard_map/all_gather | solution.py:84
  10.3 235.1 %all-reduce.7.cloned.1.call-start = ((), (), s32[]{:S(2)}) async-start(), calls=%async_computation.10 | async-start | bytes 3145728 | tf_op jit(solution)/shard_map/psum | solution.py:13
  166.5 178.5 %reduce-scatter.6.cloned.1.call-start = ((), (), s32[]{:S(2)}) async-start(), calls=%async_computation.4 | async-start | bytes 6488064 | tf_op jit(solution)/shard_map/reduce_scatter | solution.py:109
  252.0 190.1 %reduce-scatter.4.cloned.1.call-start = ((), (), s32[]{:S(2)}) async-start(), calls=%async_computation.3 | async-start | bytes 6488064 | tf_op jit(solution)/shard_map/reduce_scatter | solution.py:109
  258.7 280.7 %reduce-scatter.8.cloned.1.call-start = ((), (), s32[]{:S(2)}) async-start(), calls=%async_computation.5 | async-start | bytes 6488064 | tf_op jit(solution)/shard_map/reduce_scatter | solution.py:109
  264.4 177.7 %copy-start = (bf16[2,512,512]{2,1,0:T(8,128)(2,1)S(1)}, bf16[2,512,512]{2,1,0:T(8,128)(2,1)}, u32[]{:S(2)}) copy-start(bf16[2,512,512]{2,1,0:T(8,128)(2,1)} %param.8) | copy-start | bytes 3145732
  264.4 558.7 %all-reduce.5.cloned.1.call-start = ((), (), s32[]{:S(2)}) async-start(), calls=%async_computation.9 | async-start | bytes 10485760 | tf_op jit(solution)/shard_map/psum | solution.py:76
  443.5 100.7 %copy-start.2 = (f32[96,512]{1,0:T(8,128)S(1)}, f32[96,512]{1,0:T(8,128)}, u32[]{:S(2)}) copy-start(f32[96,512]{1,0:T(8,128)} %reduce-scatter.4.cloned.1.call-done) | copy-start | bytes 589828
  540.7 5.1 copy-start.4
  540.7 5.1 copy-start.5
  823.0 2.5 copy-start.1
  825.0 3.2 copy-start.7
  828.2 1.2 copy-start.3
  828.2 2.2 copy-start.6
Sparse Core Ops, SparseCore 0:
  11.1 51.0 all-gather.8
  65.4 47.9 all-gather.6
  116.5 47.9 all-gather.10
  167.0 78.4 all-reduce.6
  252.1 92.8 reduce-scatter.5
  348.9 93.1 reduce-scatter.3
  446.1 93.2 reduce-scatter.7
  547.8 275.1 all-reduce.4
where the time goes:
time: 843 us; the launch traced here: 842 us
  waiting for transfers between devices  747 us (89%)
  matrix products  35.6 us (4%)
  between operations  29.7 us (4%)
  other arithmetic  16.8 us (2%)
  local copies, waits for them, and re-layouts  12.5 us (1%)
    psum x1, waiting for transfers between devices, node_sums(): return lax.psum((first_part, second_part), ('row', 'col'))  275 us
    reduce_scatter x3, waiting for transfers between devices, on_device(): lax.psum_scatter(jnp.dot(columns, weights, preferred_element_type=jnp.flo...  255 us
    all_gather x3, waiting for transfers between devices, on_device(): row_slots = lax.all_gather(factor_slots[node], 'col', axis=0, tiled=True)  150 us
    psum x1, waiting for transfers between devices, spread(): return lax.psum(jnp.where(mine, shard, jnp.zeros_like(shard)), axis)  66 us
    dot_general x3, matrix products, on_device(): jnp.dot(columns, weights, preferred_element_type=jnp.float32)  18.5 us
  transfers between devices with their start and end apart: 8, of which 8 were waited for; matrix products, arithmetic and copies ran while one was open for 4% of the time, Pallas kernels for 0%

commit v1 on v0

--- a/solution.py
+++ b/solution.py
@@ -73,7 +73,7 @@
     def node_sums(node, first_part, second_part):
         if node == 0:
             return (lax.psum(first_part, ("row", "col")), None)
-        return lax.psum((first_part, second_part), ("row", "col"))
+        return lax.psum(lax.psum((first_part, second_part), "row"), "col")
 
     panels = []
     diagonals = []

time: 843 us -> 1060 us (1.26)
  waiting for transfers between devices: 747 us -> 964 us
    psum x1 -> x3, waiting for transfers between devices: 275 us -> 485 us  [the longest x1 262 us: node_sums(): return (lax.psum(first_part, ('row', 'col')), None)]
  transfers between devices with their start and end apart: 8 -> 10, of which waited for: 8 -> 10; matrix products, arithmetic and copies ran while one was open for 4% -> 4% of each run, Pallas kernels for 0% -> 0%
where the time goes in v1:
time: 1060 us
  waiting for transfers between devices  964 us (91%)
  matrix products  35.8 us (3%)
  between operations  29.5 us (3%)
  other arithmetic  15.8 us (1%)
  local copies, waits for them, and re-layouts  11.8 us (1%)
    psum x1, waiting for transfers between devices, node_sums(): return (lax.psum(first_part, ('row', 'col')), None)  262 us
    reduce_scatter x3, waiting for transfers between devices, on_device(): lax.psum_scatter(jnp.dot(columns, weights, preferred_element_type=jnp.flo...  261 us
    psum x2, waiting for transfers between devices, node_sums(): return lax.psum(lax.psum((first_part, second_part), 'row'), 'col')  223 us
    all_gather x3, waiting for transfers between devices, on_device(): row_slots = lax.all_gather(factor_slots[node], 'col', axis=0, tiled=True)  150 us
    psum x1, waiting for transfers between devices, spread(): return lax.psum(jnp.where(mine, shard, jnp.zeros_like(shard)), axis)  66 us
  transfers between devices with their start and end apart: 10, of which 10 were waited for; matrix products, arithmetic and copies ran while one was open for 4% of the time, Pallas kernels for 0%

profile of v1, /device:TPU:8, one launch (start us, length us, event | category | flops | bytes accessed | tf_op | source)
XLA Modules:
  0.0 1057.4 jit_solution(1068102721218105848)
XLA Ops:
  10.4 51.9 %all-gather.9.cloned.1.call-done = bf16[1,2048,512]{2,1,0:T(8,128)(2,1)} async-done(((bf16[1,64,512]{2,1,0:T(8,128)(2,1)}), bf16[1,2048,512]{2,1,0:T(8,128)(2,1)}) %all-gather.9.cloned.1.call-update) | async-done | bytes 2097168 | tf_op jit(solution)/shard_map/all_gather | solution.py:84
  62.3 1.9 select_bitcast_fusion.1
  64.2 49.2 %all-gather.7.cloned.1.call-done = bf16[1,2048,512]{2,1,0:T(8,128)(2,1)} async-done(((bf16[1,64,512]{2,1,0:T(8,128)(2,1)}), bf16[1,2048,512]{2,1,0:T(8,128)(2,1)}) %all-gather.7.cloned.1.call-update) | async-done | bytes 2097168 | tf_op jit(solution)/shard_map/all_gather | solution.py:84
  113.4 1.9 select_bitcast_fusion.2
  115.3 49.2 %all-gather.11.cloned.1.call-done = bf16[1,2048,512]{2,1,0:T(8,128)(2,1)} async-done(((bf16[1,64,512]{2,1,0:T(8,128)(2,1)}), bf16[1,2048,512]{2,1,0:T(8,128)(2,1)}) %all-gather.11.cloned.1.call-update) | async-done | bytes 2097168 | tf_op jit(solution)/shard_map/all_gather | solution.py:84
  164.5 1.9 select_bitcast_fusion
  172.6 6.8 constant_dynamic-slice_fusion.4
  179.4 66.0 %all-reduce.14.cloned.1.call-done = (bf16[512,512]{1,0:T(8,128)(2,1)}, bf16[512,512]{1,0:T(8,128)(2,1)}, bf16[512,512]{1,0:T(8,128)(2,1)}) async-done(((bf16[512,512]{1,0:T(8,128)(2,1)}, bf16[512,512]{1,0:T(8,128)(2,1)}, bf16[512,512]{1,0:T(8,128)(2,1)}), (bf16[512,512]{1,0:T(8,128)(2,1)}, bf16[512,512]{1,0:T(8,128)(2,1)}, bf16[512,512]{1,0:T(8,128)(2,1)})) %all-reduce.14.cloned.1.call-update) | async-done | bytes 1572880 | tf_op jit(solution)/shard_map/psum | solution.py:13
  245.4 6.5 fusion.4
  252.2 6.5 fusion
  258.8 5.5 fusion.8
  274.9 70.0 %reduce-scatter.6.cloned.1.call-done = f32[96,512]{1,0:T(8,128)} async-done(((f32[3072,512]{1,0:T(8,128)}), f32[96,512]{1,0:T(8,128)}) %reduce-scatter.6.cloned.1.call-update) | async-done | bytes 196624 | tf_op jit(solution)/shard_map/reduce_scatter | solution.py:109
  345.0 97.1 %reduce-scatter.4.cloned.1.call-done = f32[96,512]{1,0:T(8,128)} async-done(((f32[3072,512]{1,0:T(8,128)}), f32[96,512]{1,0:T(8,128)}) %reduce-scatter.4.cloned.1.call-update) | async-done | bytes 196624 | tf_op jit(solution)/shard_map/reduce_scatter | solution.py:109
  443.5 1.7 fusion.69
  445.2 94.2 %reduce-scatter.8.cloned.1.call-done = f32[96,512]{1,0:T(8,128)} async-done(((f32[3072,512]{1,0:T(8,128)}), f32[96,512]{1,0:T(8,128)}) %reduce-scatter.8.cloned.1.call-update) | async-done | bytes 196624 | tf_op jit(solution)/shard_map/reduce_scatter | solution.py:109
  540.7 1.8 fusion.67
  542.5 1.8 fusion.64
  551.6 1.7 fusion.41
  553.6 101.2 %all-reduce.12.cloned.1.call-done = (f32[512,512]{1,0:T(8,128)}, f32[512,512]{1,0:T(8,128)}, f32[512,512]{1,0:T(8,128)}, f32[512,512]{1,0:T(8,128)}) async-done(((f32[512,512]{1,0:T(8,128)}, f32[512,512]{1,0:T(8,128)}, f32[512,512]{1,0:T(8,128)}, f32[512,512]{1,0:T(8,128)}), (f32[512,512]{1,0:T(8,128)}, f32[512,512]{1,0:T(8,128)}, f32[512,512]{1,0:T(8,128)}, ...) | async-done | bytes 4194320 | tf_op jit(solution)/shard_map/psum | solution.py:76
  655.7 262.0 %all-reduce.8.cloned.1.call-done = f32[512,512]{1,0:T(8,128)} async-done(((f32[512,512]{1,0:T(8,128)}), f32[512,512]{1,0:T(8,128)}) %all-reduce.8.cloned.1.call-update) | async-done | bytes 1048592 | tf_op jit(solution)/shard_map/psum | solution.py:75
  917.7 1.8 fusion.29
  919.5 121.4 %all-reduce.10.cloned.1.call-done = (f32[512,512]{1,0:T(8,128)}, f32[512,512]{1,0:T(8,128)}, f32[512,512]{1,0:T(8,128)}, f32[512,512]{1,0:T(8,128)}) async-done(((f32[512,512]{1,0:T(8,128)}, f32[512,512]{1,0:T(8,128)}, f32[512,512]{1,0:T(8,128)}, f32[512,512]{1,0:T(8,128)}), (f32[512,512]{1,0:T(8,128)}, f32[512,512]{1,0:T(8,128)}, f32[512,512]{1,0:T(8,128)}, ...) | async-done | bytes 4194320 | tf_op jit(solution)/shard_map/psum | solution.py:76
  1040.9 2.7 fusion.13
  1048.6 2.0 pad_maximum_fusion
  (67 shorter events, 21.1 us)
Async XLA Ops:
  7.2 159.4 %copy-start.7 = (s32[3,64]{1,0:T(4,128)S(1)}, s32[3,64]{1,0:T(4,128)}, u32[]{:S(2)}) copy-start(s32[3,64]{1,0:T(4,128)} %param.7) | copy-start | bytes 2308
  7.2 55.1 %all-gather.9.cloned.1.call-start = ((), (), s32[]{:S(2)}) async-start(), calls=%async_computation.8 | async-start | bytes 2162688 | tf_op jit(solution)/shard_map/all_gather | solution.py:84
  8.8 104.6 %all-gather.7.cloned.1.call-start = ((), (), s32[]{:S(2)}) async-start(), calls=%async_computation.7 | async-start | bytes 2162688 | tf_op jit(solution)/shard_map/all_gather | solution.py:84
  9.6 154.9 %all-gather.11.cloned.1.call-start = ((), (), s32[]{:S(2)}) async-start(), calls=%async_computation.9 | async-start | bytes 2162688 | tf_op jit(solution)/shard_map/all_gather | solution.py:84
  10.3 235.1 %all-reduce.14.cloned.1.call-start = ((), (), s32[]{:S(2)}) async-start(), calls=%async_computation.12 | async-start | bytes 3145728 | tf_op jit(solution)/shard_map/psum | solution.py:13
  166.5 178.5 %reduce-scatter.6.cloned.1.call-start = ((), (), s32[]{:S(2)}) async-start(), calls=%async_computation.4 | async-start | bytes 6488064 | tf_op jit(solution)/shard_map/reduce_scatter | solution.py:109
  252.0 190.1 %reduce-scatter.4.cloned.1.call-start = ((), (), s32[]{:S(2)}) async-start(), calls=%async_computation.3 | async-start | bytes 6488064 | tf_op jit(solution)/shard_map/reduce_scatter | solution.py:109
  258.7 280.7 %reduce-scatter.8.cloned.1.call-start = ((), (), s32[]{:S(2)}) async-start(), calls=%async_computation.5 | async-start | bytes 6488064 | tf_op jit(solution)/shard_map/reduce_scatter | solution.py:109
  264.3 177.8 %copy-start = (bf16[2,512,512]{2,1,0:T(8,128)(2,1)S(1)}, bf16[2,512,512]{2,1,0:T(8,128)(2,1)}, u32[]{:S(2)}) copy-start(bf16[2,512,512]{2,1,0:T(8,128)(2,1)} %param.8) | copy-start | bytes 3145732
  264.4 390.5 %all-reduce.12.cloned.1.call-start = ((), (), s32[]{:S(2)}) async-start(), calls=%async_computation.11 | async-start | bytes 8388608 | tf_op jit(solution)/shard_map/psum | solution.py:76
  443.5 100.7 %copy-start.3 = (f32[96,512]{1,0:T(8,128)S(1)}, f32[96,512]{1,0:T(8,128)}, u32[]{:S(2)}) copy-start(f32[96,512]{1,0:T(8,128)} %reduce-scatter.4.cloned.1.call-done) | copy-start | bytes 589828
  545.9 371.7 %all-reduce.8.cloned.1.call-start = ((), (), s32[]{:S(2)}) async-start(), calls=%async_computation.6 | async-start | bytes 2097152 | tf_op jit(solution)/shard_map/psum | solution.py:75
  553.3 487.6 %all-reduce.10.cloned.1.call-start = ((), (), s32[]{:S(2)}) async-start(), calls=%async_computation.10 | async-start | bytes 8388608 | tf_op jit(solution)/shard_map/psum | solution.py:76
  917.7 123.3 %copy-start.2 = (f32[512,512]{1,0:T(8,128)S(1)}, f32[512,512]{1,0:T(8,128)}, u32[]{:S(2)}) copy-start(f32[512,512]{1,0:T(8,128)} %all-reduce.8.cloned.1.call-done) | copy-start | bytes 3145732
  1040.9 2.7 copy-start.1
  1040.9 2.8 copy-start.6
  1043.7 1.2 copy-start.4
  1043.7 2.2 copy-start.5
Sparse Core Ops, SparseCore 0:
  11.1 51.0 all-gather.8
  65.4 47.9 all-gather.6
  116.5 47.9 all-gather.10
  167.0 78.4 all-reduce.13
  252.1 92.8 reduce-scatter.5
  348.9 93.1 reduce-scatter.3
  446.1 93.2 reduce-scatter.7
  546.1 108.7 all-reduce.11
  660.3 257.3 all-reduce.7
  921.0 119.8 all-reduce.9
